TPU v7x, 128 devices: a whole 4x4x4 slice. The times are simulated.
128 devices in a mesh: seq: 16 (over z, x), hid: 4 (over y), rep: 2 (over core).
Axes of the slice: x: 4, y: 4, z: 4, core: 2. Of those that a mesh axis runs over, the one named last changes fastest.
Arguments:
- tokens: bfloat16 [16384, 5376], P(('rep', 'seq'), 'hid'), parts along dimension 0, may hold values from -6 to 6
- norm_gain: float32 [5376], replicated, may hold values from 0.1 to 1.9
- w_query: bfloat16 [5376, 4096], P('seq', 'hid'), may hold values from -0.078125 to 0.078125
- w_key: bfloat16 [5376, 2048], P('seq', 'hid'), may hold values from -0.078125 to 0.078125
- w_value: bfloat16 [5376, 2048], P('seq', 'hid'), may hold values from -0.078125 to 0.078125
- query_gain: float32 [128], replicated, may hold values from 0.5 to 8
- key_gain: float32 [128], replicated, may hold values from 0.5 to 8
- w_out: bfloat16 [4096, 5376], P('hid', 'seq'), may hold values from -0.09375 to 0.09375
Outputs:
- attended: bfloat16 [16384, 5376], P(('rep', 'seq'), 'hid'), parts along dimension 0
There are 2 independent parts, one for each index of `rep`. A program takes and returns all parts, laid end to end along the dimension named above; an argument that names none is the same for every part. Nothing has to cross between parts.
All inputs are finite; a program needn't handle non-finite values.
Results may differ from a plain program's by a relative error of at most 0.023.
The roundings to bfloat16 on the way count: a program that leaves them out, or rounds other values in their place, can miss the bound.
Values may be sent and summed in bfloat16 or wider, within the bound.
A program may use at most 128 MiB of HBM per device.

v0:
```python
import jax
import jax.numpy as jnp
from jax import lax
from jax.sharding import PartitionSpec as P

HEAD_WIDTH = 128
WINDOW = 1024
QSCALE = 168
DEPTH = 2


def shifted(x, axis, by):
    count = lax.axis_size(axis)
    pairs = [(i, i + by) for i in range(count) if 0 <= i + by < count]
    return lax.ppermute(x, axis, pairs)


def rope(heads, positions):
    half = heads.shape[-1] // 2
    freq = 10000.0 ** (-(jnp.arange(half, dtype=jnp.float32) * 2.0) / heads.shape[-1])
    angle = positions[:, None] * freq[None, :]
    cosine = jnp.cos(angle)[:, None, :]
    sine = jnp.sin(angle)[:, None, :]
    first = heads[..., :half]
    second = heads[..., half:]
    return jnp.concatenate(
        [first * cosine - second * sine, second * cosine + first * sine], axis=-1
    )


def head_norm(heads, gain):
    return heads * lax.rsqrt(jnp.mean(heads * heads, axis=-1, keepdims=True) + 1e-06) * gain


def add_rows(normed, piece):
    return jnp.dot(normed, piece, preferred_element_type=jnp.float32)


def shards(tokens, norm_gain, w_query, w_key, w_value, query_gain, key_gain, w_out):
    whole = lax.all_gather(tokens, "hid", axis=1, tiled=True)
    xfloat = whole.astype(jnp.float32)
    normed = (
        xfloat * lax.rsqrt(jnp.mean(xfloat * xfloat, axis=-1, keepdims=True) + 1e-06) * norm_gain
    ).astype(jnp.bfloat16)
    rows = normed.shape[0]

    def add_one(piece):
        return add_rows(normed, piece)

    query = add_one(lax.all_gather(w_query, "seq", axis=0, tiled=True))
    key = add_one(lax.all_gather(w_key, "seq", axis=0, tiled=True))
    value = add_one(lax.all_gather(w_value, "seq", axis=0, tiled=True))
    local_heads = w_query.shape[1] // HEAD_WIDTH
    local_kv = w_key.shape[1] // HEAD_WIDTH
    base = lax.axis_index("seq") * rows
    qpos = base + jnp.arange(rows, dtype=jnp.int32)
    positions = qpos.astype(jnp.float32)
    qh = (
        rope(head_norm(query.reshape(rows, local_heads, HEAD_WIDTH), query_gain), positions)
        * QSCALE ** (-0.5)
    ).astype(jnp.bfloat16)
    kh = rope(head_norm(key.reshape(rows, local_kv, HEAD_WIDTH), key_gain), positions).astype(
        jnp.bfloat16
    )
    value_head = value.reshape(rows, local_kv, HEAD_WIDTH).astype(jnp.bfloat16)
    key_blocks = []
    value_blocks = []
    for distance in range(1, DEPTH + 1):
        arrived = shifted((kh, value_head), "seq", distance)
        key_blocks.insert(0, arrived[0])
        value_blocks.insert(0, arrived[1])
    keys = jnp.concatenate(key_blocks + [kh], axis=0)
    values = jnp.concatenate(value_blocks + [value_head], axis=0)
    window_extent = keys.shape[0]
    kpos = base - DEPTH * rows + jnp.arange(window_extent, dtype=jnp.int32)
    diff = qpos[:, None] - kpos[None, :]
    allowed = (diff >= 0) & (diff < WINDOW) & (kpos >= 0)[None, :]
    group = local_heads // local_kv
    grouped = qh.reshape(rows, local_kv, group, HEAD_WIDTH).transpose(1, 0, 2, 3)

    def one_head(operands):
        qpart, kpart, vpart = operands
        scores = jnp.einsum("rgd,ld->grl", qpart, kpart, preferred_element_type=jnp.float32)
        scores = jnp.where(allowed[None], scores, -jnp.inf)
        probs = jax.nn.softmax(scores, axis=-1).astype(jnp.bfloat16)
        mixed = jnp.einsum("grl,ld->rgd", probs, vpart, preferred_element_type=jnp.float32)
        return mixed.astype(jnp.bfloat16)

    per_head = lax.map(one_head, (grouped, keys.transpose(1, 0, 2), values.transpose(1, 0, 2)))
    heads_out = per_head.transpose(1, 0, 2, 3).reshape(rows, local_heads * HEAD_WIDTH)
    terms = jnp.dot(
        heads_out,
        lax.all_gather(w_out, "seq", axis=1, tiled=True),
        preferred_element_type=jnp.float32,
    )
    return lax.psum_scatter(terms.astype(jnp.bfloat16), "hid", scatter_dimension=1, tiled=True)


def solution(mesh):
    return jax.shard_map(
        shards,
        mesh=mesh,
        in_specs=(
            P(("rep", "seq"), "hid"),
            P(),
            P("seq", "hid"),
            P("seq", "hid"),
            P("seq", "hid"),
            P(),
            P(),
            P("hid", "seq"),
        ),
        out_specs=P(("rep", "seq"), "hid"),
        check_vma=False,
    )
```

profile of v0, /device:TPU:1, one launch (start us, length us, event | category | flops | bytes accessed | tf_op | source)
XLA Modules:
  0.0 466.9 jit_solution(10605443407271170900)
XLA Ops:
  6.5 0.7 all-gather.6.cloned.1.call-update
  7.3 0.7 all-gather.10.cloned.1.call-update
  8.1 0.7 all-gather.8.cloned.1.call-update
  8.8 0.5 all-gather.12.cloned.1.call-update
  9.4 0.5 all-gather.14.cloned.1.call-update
  10.0 1.0 multiply_cosine_fusion
  11.0 60.4 %all-gather.6.cloned.1.call-done = bf16[512,5376]{0,1:T(8,128)(2,1)} async-done(((bf16[512,1344]{0,1:T(8,128)(2,1)}), bf16[512,5376]{0,1:T(8,128)(2,1)}) %all-gather.6.cloned.1.call-update) | async-done | bytes 5505040 | tf_op jit(solution)/shard_map/all_gather | solution.py:40
  71.4 3.8 fusion.41
  75.2 56.7 %all-gather.10.cloned.1.call-done = bf16[5376,512]{1,0:T(8,128)(2,1)} async-done(((bf16[336,512]{1,0:T(8,128)(2,1)}), bf16[5376,512]{1,0:T(8,128)(2,1)}) %all-gather.10.cloned.1.call-update) | async-done | bytes 5505040 | tf_op jit(solution)/shard_map/all_gather | solution.py:51
  131.9 7.6 %multiply_reduce_fusion.1 = (f32[512,4]{0,1:T(4,128)S(1)}, f32[512,512]{0,1:T(8,128)S(1)}) fusion(bf16[5376,512]{1,0:T(8,128)(2,1)} %all-gather.10.cloned.1.call-done, bf16[512,5376]{0,1:T(8,128)(2,1)} %all-gather.6.cloned.1.call-done, f32[5376]{0:T(1024)S(1)} %copy-done.2, f32[512]{0:T(512)S(1)} %add_rsqrt_fusion.2), kind=kOutput, calls=%fused_computation.52 | convolution fusion | flops 2830104576 | bytes 12090368 | tf_op jit(solution)/shard_map/dot_general | solution.py:36
  139.9 0.3 multiply_multiply_fusion.1
  140.2 0.5 subtract_convert_fusion
  141.0 4.6 collective-permute-start.2
  145.6 2.2 collective-permute-start.3
  147.9 54.8 %all-gather.8.cloned.1.call-done = bf16[5376,512]{1,0:T(8,128)(2,1)} async-done(((bf16[336,512]{1,0:T(8,128)(2,1)}), bf16[5376,512]{1,0:T(8,128)(2,1)}) %all-gather.8.cloned.1.call-update) | async-done | bytes 5505040 | tf_op jit(solution)/shard_map/all_gather | solution.py:52
  202.7 8.4 %convolution_convert_fusion.1 = bf16[512,512]{0,1:T(8,128)(2,1)} fusion(bf16[5376,512]{1,0:T(8,128)(2,1)} %all-gather.8.cloned.1.call-done, bf16[512,5376]{0,1:T(8,128)(2,1)} %all-gather.6.cloned.1.call-done, f32[5376]{0:T(1024)S(1)} %copy-done.2, f32[512]{0:T(512)S(1)} %add_rsqrt_fusion.2), kind=kOutput, calls=%fused_computation.47 | convolution fusion | flops 2829844480 | bytes 11557888 | tf_op jit(solution)/shard_map/dot_general | solution.py:36
  211.1 5.4 %collective-permute-start = (bf16[512,4,128]{0,2,1:T(8,128)(2,1)}, bf16[512,4,128]{0,2,1:T(8,128)(2,1)}, u32[]{:S(2)}, u32[]{:S(2)}) collective-permute-start(bf16[512,4,128]{0,2,1:T(8,128)(2,1)} %bitcast), channel_id=1, source_target_pairs={{0,16},{8,24},{16,32},{24,40},{32,48},{40,56},{48,64},{56,72},{64,... | collective-permute-start | bytes 1572872 | tf_op jit(solution)/shard_map/ppermute | solution.py:15
  216.5 3.0 collective-permute-start.1
  219.6 1.5 maximum_bitcast_fusion.1
  221.1 12.3 %collective-permute-done = bf16[512,4,128]{0,2,1:T(8,128)(2,1)} collective-permute-done((bf16[512,4,128]{0,2,1:T(8,128)(2,1)}, bf16[512,4,128]{0,2,1:T(8,128)(2,1)}, u32[]{:S(2)}, u32[]{:S(2)}) %collective-permute-start) | collective-permute-done | bytes 524320 | tf_op jit(solution)/shard_map/ppermute | solution.py:15
  233.4 15.0 %collective-permute-done.1 = bf16[512,4,128]{0,2,1:T(8,128)(2,1)} collective-permute-done((bf16[512,4,128]{0,2,1:T(8,128)(2,1)}, bf16[512,4,128]{0,2,1:T(8,128)(2,1)}, u32[]{:S(2)}, u32[]{:S(2)}) %collective-permute-start.1) | collective-permute-done | bytes 524320 | tf_op jit(solution)/shard_map/ppermute | solution.py:15
  248.5 2.6 maximum_bitcast_fusion
  251.0 55.3 %all-gather.12.cloned.1.call-done = bf16[5376,1024]{1,0:T(8,128)(2,1)} async-done(((bf16[336,1024]{1,0:T(8,128)(2,1)}), bf16[5376,1024]{1,0:T(8,128)(2,1)}) %all-gather.12.cloned.1.call-update) | async-done | bytes 11010064 | tf_op jit(solution)/shard_map/all_gather | solution.py:50
  306.4 11.7 %convolution_bitcast_fusion = f32[64,8,8,128]{3,1,2,0:T(8,128)S(1)} fusion(bf16[5376,1024]{1,0:T(8,128)(2,1)} %all-gather.12.cloned.1.call-done, bf16[512,5376]{0,1:T(8,128)(2,1)} %all-gather.6.cloned.1.call-done, f32[5376]{0:T(1024)S(1)} %copy-done.2, f32[512]{0:T(512)S(1)} %add_rsqrt_fusion.2), kind=kOutput, calls=%fused_computation.44 | convolution fusion | flops 5648154624 | bytes 18635776 | tf_op jit(solution)/shard_map/dot_general | solution.py:36
  318.1 0.5 copy.25
  318.6 0.6 multiply_reduce_fusion
  319.4 0.9 multiply_multiply_fusion
  320.3 1.2 multiply_subtract_fusion
  321.5 0.4 copy.22
  321.9 0.4 copy.23
  322.4 0.6 fusion.45
  323.0 0.6 copy-done.3
  323.6 43.2 %while.11 = (s32[]{:T(128)}, bf16[4,512,2,128]{1,3,2,0:T(8,128)(2,1)S(1)}, bf16[4,1536,128]{1,2,0:T(8,128)(2,1)}, bf16[4,1536,128]{2,1,0:T(8,128)(2,1)}, bf16[4,...) while((s32[]{:T(128)}, ...), condition=%wide.region_6.7_spmd.clone, body=%wide.region_3.6_spmd.clone.sunk | while | flops 817235456 | bytes 15486557 | solution.py:89
  323.6 1.2 fusion.74
  324.8 5.8 %fusion.75 = (f32[2,512]{1,0:T(2,128)S(1)}, f32[2,512,1536]{1,2,0:T(8,128)}) fusion(pred[512,1536]{0,1:T(8,128)(4,1)S(1)} %fusion.74, bf16[4,1536,128]{2,1,0:T(8,128)(2,1)} %get-tuple-element.159, s32[]{:T(128)} %get-tuple-element.147, bf16[4,512,2,128]{3,1,2,0:T(8,128)(2,1)S(1)} %get-tuple-element.160), kind=kOutput, calls=%fused_computation.65.clone.1 | convolution fusion | flops 407373312 | bytes 7738368 | tf_op jit(solution)/shard_map/while/body/eval_jaxpr/sub | solution.py:85
  330.6 3.6 fusion.76
  334.2 1.2 fusion.74
  335.4 5.8 %fusion.75 = (f32[2,512]{1,0:T(2,128)S(1)}, f32[2,512,1536]{1,2,0:T(8,128)}) fusion(pred[512,1536]{0,1:T(8,128)(4,1)S(1)} %fusion.74, bf16[4,1536,128]{2,1,0:T(8,128)(2,1)} %get-tuple-element.159, s32[]{:T(128)} %get-tuple-element.147, bf16[4,512,2,128]{3,1,2,0:T(8,128)(2,1)S(1)} %get-tuple-element.160), kind=kOutput, calls=%fused_computation.65.clone.1 | convolution fusion | flops 407373312 | bytes 7738368 | tf_op jit(solution)/shard_map/while/body/eval_jaxpr/sub | solution.py:85
  341.2 4.3 fusion.76
  345.6 1.2 fusion.74
  346.8 5.8 %fusion.75 = (f32[2,512]{1,0:T(2,128)S(1)}, f32[2,512,1536]{1,2,0:T(8,128)}) fusion(pred[512,1536]{0,1:T(8,128)(4,1)S(1)} %fusion.74, bf16[4,1536,128]{2,1,0:T(8,128)(2,1)} %get-tuple-element.159, s32[]{:T(128)} %get-tuple-element.147, bf16[4,512,2,128]{3,1,2,0:T(8,128)(2,1)S(1)} %get-tuple-element.160), kind=kOutput, calls=%fused_computation.65.clone.1 | convolution fusion | flops 407373312 | bytes 7738368 | tf_op jit(solution)/shard_map/while/body/eval_jaxpr/sub | solution.py:85
  352.6 3.6 fusion.76
  356.2 1.2 fusion.74
  357.4 5.8 %fusion.75 = (f32[2,512]{1,0:T(2,128)S(1)}, f32[2,512,1536]{1,2,0:T(8,128)}) fusion(pred[512,1536]{0,1:T(8,128)(4,1)S(1)} %fusion.74, bf16[4,1536,128]{2,1,0:T(8,128)(2,1)} %get-tuple-element.159, s32[]{:T(128)} %get-tuple-element.147, bf16[4,512,2,128]{3,1,2,0:T(8,128)(2,1)S(1)} %get-tuple-element.160), kind=kOutput, calls=%fused_computation.65.clone.1 | convolution fusion | flops 407373312 | bytes 7738368 | tf_op jit(solution)/shard_map/while/body/eval_jaxpr/sub | solution.py:85
  363.2 3.5 fusion.76
  366.8 24.1 %all-gather.14.cloned.1.call-done = bf16[1024,5376]{0,1:T(8,128)(2,1)} async-done(((bf16[1024,336]{0,1:T(8,128)(2,1)}), bf16[1024,5376]{0,1:T(8,128)(2,1)}) %all-gather.14.cloned.1.call-update) | async-done | bytes 11010064 | tf_op jit(solution)/shard_map/all_gather | solution.py:93
  390.9 11.8 %convolution_convert_fusion = bf16[512,5376]{0,1:T(8,128)(2,1)} fusion(bf16[1024,5376]{0,1:T(8,128)(2,1)} %all-gather.14.cloned.1.call-done, bf16[512,1024]{0,1:T(8,128)(2,1)S(1)} %bitcast.83), kind=kOutput, calls=%fused_computation.37 | convolution fusion | flops 5639897088 | bytes 17563648 | tf_op jit(solution)/shard_map/dot_general | solution.py:91
  402.7 57.3 %reduce-scatter.2.cloned.1.call-done = bf16[512,1344]{0,1:T(8,128)(2,1)} async-done(((bf16[512,5376]{0,1:T(8,128)(2,1)}), bf16[512,1344]{0,1:T(8,128)(2,1)}) %reduce-scatter.2.cloned.1.call-update) | async-done | bytes 1376272 | tf_op jit(solution)/shard_map/reduce_scatter | solution.py:96
  (29 shorter events, 1.1 us)
Async XLA Ops:
  6.5 64.9 %all-gather.6.cloned.1.call-start = ((), (), s32[]{:S(2)}) async-start(), calls=%async_computation.1 | async-start | bytes 6881280 | tf_op jit(solution)/shard_map/all_gather | solution.py:40
  7.3 124.7 %all-gather.10.cloned.1.call-start = ((), (), s32[]{:S(2)}) async-start(), calls=%async_computation.3 | async-start | bytes 5849088 | tf_op jit(solution)/shard_map/all_gather | solution.py:51
  8.0 194.7 %all-gather.8.cloned.1.call-start = ((), (), s32[]{:S(2)}) async-start(), calls=%async_computation.2 | async-start | bytes 5849088 | tf_op jit(solution)/shard_map/all_gather | solution.py:52
  8.7 297.6 %all-gather.12.cloned.1.call-start = ((), (), s32[]{:S(2)}) async-start(), calls=%async_computation.4 | async-start | bytes 11698176 | tf_op jit(solution)/shard_map/all_gather | solution.py:50
  9.3 381.6 %all-gather.14.cloned.1.call-start = ((), (), s32[]{:S(2)}) async-start(), calls=%async_computation.5 | async-start | bytes 11698176 | tf_op jit(solution)/shard_map/all_gather | solution.py:93
  9.9 122.0 %copy-start.2 = (f32[5376]{0:T(1024)S(1)}, f32[5376]{0:T(1024)}, u32[]{:S(2)}) copy-start(f32[5376]{0:T(1024)} %param.11) | copy-start | bytes 64516
  9.9 450.1 %reduce-scatter.2.cloned.1.call-start = ((), (), s32[]{:S(2)}) async-start(), calls=%async_computation.6 | async-start | bytes 6881280 | tf_op jit(solution)/shard_map/reduce_scatter | solution.py:96
  75.2 64.7 %copy-start = (f32[128]{0:T(128)S(1)}, f32[128]{0:T(128)}, u32[]{:S(2)}) copy-start(f32[128]{0:T(128)} %param.16) | copy-start | bytes 1540
  141.0 78.6 %collective-permute-start.2 = (bf16[512,4,128]{2,0,1:T(8,128)(2,1)S(1)}, bf16[512,4,128]{2,0,1:T(8,128)(2,1)S(1)}, u32[]{:S(2)}, u32[]{:S(2)}) collective-permute-start(bf16[512,4,128]{2,0,1:T(8,128)(2,1)S(1)} %pad_maximum_fusion), channel_id=1, source_target_pairs={{0,16},{8,24},{16,32},{24,40},{32,48},{40,56},{48,64},{56,72},{64,... | collective-permute-start | bytes 1572872 | tf_op jit(solution)/shard_map/ppermute | solution.py:15
  145.6 73.9 %collective-permute-start.3 = (bf16[512,4,128]{2,0,1:T(8,128)(2,1)S(1)}, bf16[512,4,128]{2,0,1:T(8,128)(2,1)S(1)}, u32[]{:S(2)}, u32[]{:S(2)}) collective-permute-start(bf16[512,4,128]{2,0,1:T(8,128)(2,1)S(1)} %pad_maximum_fusion), channel_id=1, source_target_pairs={{0,8},{8,16},{16,24},{24,32},{32,40},{40,48},{48,56},{56,64},{64,7... | collective-permute-start | bytes 1572872 | tf_op jit(solution)/shard_map/ppermute | solution.py:15
  211.1 22.3 %collective-permute-start = (bf16[512,4,128]{0,2,1:T(8,128)(2,1)}, bf16[512,4,128]{0,2,1:T(8,128)(2,1)}, u32[]{:S(2)}, u32[]{:S(2)}) collective-permute-start(bf16[512,4,128]{0,2,1:T(8,128)(2,1)} %bitcast), channel_id=1, source_target_pairs={{0,16},{8,24},{16,32},{24,40},{32,48},{40,56},{48,64},{56,72},{64,... | collective-permute-start | bytes 1572872 | tf_op jit(solution)/shard_map/ppermute | solution.py:15
  216.5 31.9 %collective-permute-start.1 = (bf16[512,4,128]{0,2,1:T(8,128)(2,1)}, bf16[512,4,128]{0,2,1:T(8,128)(2,1)}, u32[]{:S(2)}, u32[]{:S(2)}) collective-permute-start(bf16[512,4,128]{0,2,1:T(8,128)(2,1)} %bitcast), channel_id=1, source_target_pairs={{0,8},{8,16},{16,24},{24,32},{32,40},{40,48},{48,56},{56,64},{64,7... | collective-permute-start | bytes 1572872 | tf_op jit(solution)/shard_map/ppermute | solution.py:15
  318.1 1.4 copy-start.1
  322.3 1.2 copy-start.3
Sparse Core Ops, SparseCore 0:
  9.0 62.3 all-gather.5
  73.5 58.3 all-gather.9
  134.1 68.5 all-gather.7
  204.7 101.6 all-gather.11
  308.3 82.4 all-gather.13
  402.8 57.1 reduce-scatter.1
where the time goes:
time: 467 us
  waiting for transfers between devices  339 us (73%)
  matrix products  77.8 us (17%)
  other arithmetic  18.1 us (4%)
  starting transfers between devices  15.5 us (3%)
  between operations  13.7 us (3%)
    all_gather x1, waiting for transfers between devices, shards(): whole = lax.all_gather(tokens, 'hid', axis=1, tiled=True)  60.4 us
    reduce_scatter x1, waiting for transfers between devices, shards(): lax.psum_scatter(terms.astype(jnp.bfloat16), 'hid', scatter_dimension=1,...  57.3 us
    all_gather x1, waiting for transfers between devices, shards(): key = add_one(lax.all_gather(w_key, 'seq', axis=0, tiled=True))  56.7 us
    all_gather x1, waiting for transfers between devices, shards(): query = add_one(lax.all_gather(w_query, 'seq', axis=0, tiled=True))  55.3 us
    all_gather x1, waiting for transfers between devices, shards(): value = add_one(lax.all_gather(w_value, 'seq', axis=0, tiled=True))  54.8 us
    dot_general x3, matrix products, add_rows(): return jnp.dot(normed, piece, preferred_element_type=jnp.float32)  27.7 us
    ppermute x4, waiting for transfers between devices, shifted(): return lax.ppermute(x, axis, pairs)  27.4 us
    all_gather x1, waiting for transfers between devices, shards(): lax.all_gather(w_out, 'seq', axis=1, tiled=True)  24.1 us
  transfers between devices with their start and end apart: 10, of which 8 were waited for; matrix products, arithmetic and copies ran while one was open for 18% of the time, Pallas kernels for 0%

commit v1 on v0

--- a/solution.py
+++ b/solution.py
@@ -49,7 +49,48 @@
 
     query = add_one(lax.all_gather(w_query, "seq", axis=0, tiled=True))
     key = add_one(lax.all_gather(w_key, "seq", axis=0, tiled=True))
-    value = add_one(lax.all_gather(w_value, "seq", axis=0, tiled=True))
+
+    def register_yards(dimension_no, x_local):
+        named_axis = "seq"
+        r_now, e_next, heard = (
+            jax.lax.psum(1, named_axis),
+            jax.lax.axis_index(named_axis),
+            x_local.shape[dimension_no],
+        )
+        current_value = lax.dynamic_update_slice_in_dim(
+            jnp.zeros(
+                [
+                    dd * r_now if hop_no == dimension_no else dd
+                    for hop_no, dd in enumerate(x_local.shape)
+                ],
+                x_local.dtype,
+            ),
+            x_local,
+            e_next * heard,
+            axis=dimension_no,
+        )
+        x_now = row_out = x_local
+        for dev in range(1, r_now // 2 + 1):
+            x_now = jax.lax.ppermute(
+                x_now,
+                named_axis,
+                perm=list(map(lambda hop_no: (hop_no, (hop_no + 1) % r_now), range(r_now))),
+            )
+            current_value = lax.dynamic_update_slice_in_dim(
+                current_value, x_now, (e_next - dev) % r_now * heard, axis=dimension_no
+            )
+            if 2 * dev < r_now:
+                row_out = jax.lax.ppermute(
+                    row_out,
+                    named_axis,
+                    list(map(lambda hop_no: (hop_no, (hop_no - 1) % r_now), range(r_now))),
+                )
+                current_value = lax.dynamic_update_slice_in_dim(
+                    current_value, row_out, (e_next + dev) % r_now * heard, axis=dimension_no
+                )
+        return current_value
+
+    value = add_one(register_yards(0, w_value))
     local_heads = w_query.shape[1] // HEAD_WIDTH
     local_kv = w_key.shape[1] // HEAD_WIDTH
     base = lax.axis_index("seq") * rows

time: 467 us -> 415 us (0.89)
  waiting for transfers between devices: 339 us -> 235 us
  starting transfers between devices: 15.5 us -> 51.6 us
  local copies, waits for them, and re-layouts: 2.44 us -> 17.1 us
    all_gather x1, waiting for transfers between devices: 60.4 us -> 0.01 us  [shards(): whole = lax.all_gather(tokens, 'hid', axis=1, tiled=True)]
    all_gather x1 -> x0, waiting for transfers between devices: 54.8 us -> none  [shards(): value = add_one(lax.all_gather(w_value, 'seq', axis=0, tiled=True))]
    ppermute x0 -> x15, waiting for transfers between devices: none -> 38.5 us  [the longest x8 28.4 us: register_yards(): jax.lax.ppermute(x_now, named_axis, perm=list(map(lambda hop_no: (hop_no,...]
    ppermute x0 -> x15, starting transfers between devices: none -> 37 us  [the longest x7 34.9 us: register_yards(): jax.lax.ppermute(row_out, named_axis, list(map(lambda hop_no: (hop_no, (h...]
    all_gather x1, waiting for transfers between devices: 56.7 us -> 33.9 us  [shards(): key = add_one(lax.all_gather(w_key, 'seq', axis=0, tiled=True))]
    dynamic_update_slice x0 -> x16, local copies, waits for them, and re-layouts: none -> 12.1 us  [the longest x8 6.08 us: register_yards(): lax.dynamic_update_slice_in_dim(current_value, x_now, (e_next - dev) % r_...]
  transfers between devices with their start and end apart: 10 -> 24, of which waited for: 8 -> 14; matrix products, arithmetic and copies ran while one was open for 18% -> 25% of each run, Pallas kernels for 0% -> 0%
where the time goes in v1:
time: 415 us; the launch traced here: 414 us
  waiting for transfers between devices  235 us (57%)
  matrix products  78.2 us (19%)
  starting transfers between devices  51.6 us (12%)
  other arithmetic  18.4 us (4%)
  local copies, waits for them, and re-layouts  17.1 us (4%)
  between operations  13.7 us (3%)
    reduce_scatter x1, waiting for transfers between devices, shards(): lax.psum_scatter(terms.astype(jnp.bfloat16), 'hid', scatter_dimension=1,...  57.3 us
    all_gather x1, waiting for transfers between devices, shards(): query = add_one(lax.all_gather(w_query, 'seq', axis=0, tiled=True))  54.9 us
    ppermute x7, starting transfers between devices, register_yards(): jax.lax.ppermute(row_out, named_axis, list(map(lambda hop_no: (hop_no, (h...  34.9 us
    all_gather x1, waiting for transfers between devices, shards(): key = add_one(lax.all_gather(w_key, 'seq', axis=0, tiled=True))  33.9 us
    ppermute x8, waiting for transfers between devices, register_yards(): jax.lax.ppermute(x_now, named_axis, perm=list(map(lambda hop_no: (hop_no,...  28.4 us
    ppermute x4, waiting for transfers between devices, shifted(): return lax.ppermute(x, axis, pairs)  27 us
    dot_general x3, matrix products, add_rows(): return jnp.dot(normed, piece, preferred_element_type=jnp.float32)  26.1 us
    sub x4, matrix products, one_head(): probs = jax.nn.softmax(scores, axis=-1).astype(jnp.bfloat16)  23.4 us
  transfers between devices with their start and end apart: 24, of which 14 were waited for; matrix products, arithmetic and copies ran while one was open for 25% of the time, Pallas kernels for 0%

profile of v1, /device:TPU:1, one launch (start us, length us, event | category | flops | bytes accessed | tf_op | source)
XLA Modules:
  0.0 414.5 jit_solution(12328304477273658841)
XLA Ops:
  9.4 2.1 collective-permute-start
  11.5 4.8 %collective-permute-start.1 = (bf16[336,512]{1,0:T(8,128)(2,1)}, bf16[336,512]{1,0:T(8,128)(2,1)S(1)}, u32[]{:S(2)}, u32[]{:S(2)}) collective-permute-start(bf16[336,512]{1,0:T(8,128)(2,1)} %param.14), channel_id=1, source_target_pairs={{0,120},{8,0},{16,8},{24,16},{32,24},{40,32},{48,40},{56,48},{64,5... | collective-permute-start | bytes 1032200 | tf_op jit(solution)/shard_map/ppermute | solution.py:83
  16.3 7.9 %collective-permute-done = bf16[336,512]{1,0:T(8,128)(2,1)S(1)} collective-permute-done((bf16[336,512]{1,0:T(8,128)(2,1)}, bf16[336,512]{1,0:T(8,128)(2,1)S(1)}, u32[]{:S(2)}, u32[]{:S(2)}) %collective-permute-start) | collective-permute-done | bytes 344096 | tf_op jit(solution)/shard_map/ppermute | solution.py:74
  24.2 4.8 %collective-permute-start.3 = (bf16[336,512]{1,0:T(8,128)(2,1)S(1)}, bf16[336,512]{1,0:T(8,128)(2,1)S(1)}, u32[]{:S(2)}, u32[]{:S(2)}) collective-permute-start(bf16[336,512]{1,0:T(8,128)(2,1)S(1)} %collective-permute-done.1), channel_id=1, source_target_pairs={{0,120},{8,0},{16,8},{24,16},{32,24},{40,32},{48,40},{56,48},{64,5... | collective-permute-start | bytes 1032200 | tf_op jit(solution)/shard_map/ppermute | solution.py:83
  29.0 6.9 %collective-permute-done.2 = bf16[336,512]{1,0:T(8,128)(2,1)S(1)} collective-permute-done((bf16[336,512]{1,0:T(8,128)(2,1)S(1)}, bf16[336,512]{1,0:T(8,128)(2,1)S(1)}, u32[]{:S(2)}, u32[]{:S(2)}) %collective-permute-start.2) | collective-permute-done | bytes 344096 | tf_op jit(solution)/shard_map/ppermute | solution.py:74
  35.9 4.8 %collective-permute-start.5 = (bf16[336,512]{1,0:T(8,128)(2,1)S(1)}, bf16[336,512]{1,0:T(8,128)(2,1)S(1)}, u32[]{:S(2)}, u32[]{:S(2)}) collective-permute-start(bf16[336,512]{1,0:T(8,128)(2,1)S(1)} %collective-permute-done.3), channel_id=1, source_target_pairs={{0,120},{8,0},{16,8},{24,16},{32,24},{40,32},{48,40},{56,48},{64,5... | collective-permute-start | bytes 1032200 | tf_op jit(solution)/shard_map/ppermute | solution.py:83
  42.0 4.6 %collective-permute-done.4 = bf16[336,512]{1,0:T(8,128)(2,1)S(1)} collective-permute-done((bf16[336,512]{1,0:T(8,128)(2,1)S(1)}, bf16[336,512]{1,0:T(8,128)(2,1)S(1)}, u32[]{:S(2)}, u32[]{:S(2)}) %collective-permute-start.4) | collective-permute-done | bytes 344096 | tf_op jit(solution)/shard_map/ppermute | solution.py:74
  46.6 2.8 broadcast_in_dim.16
  50.9 4.8 %collective-permute-start.7 = (bf16[336,512]{1,0:T(8,128)(2,1)S(1)}, bf16[336,512]{1,0:T(8,128)(2,1)S(1)}, u32[]{:S(2)}, u32[]{:S(2)}) collective-permute-start(bf16[336,512]{1,0:T(8,128)(2,1)S(1)} %collective-permute-done.5), channel_id=1, source_target_pairs={{0,120},{8,0},{16,8},{24,16},{32,24},{40,32},{48,40},{56,48},{64,5... | collective-permute-start | bytes 1032200 | tf_op jit(solution)/shard_map/ppermute | solution.py:83
  58.0 1.9 collective-permute-done.7
  59.9 5.2 %collective-permute-start.9 = (bf16[336,512]{1,0:T(8,128)(2,1)S(1)}, bf16[336,512]{1,0:T(8,128)(2,1)S(1)}, u32[]{:S(2)}, u32[]{:S(2)}) collective-permute-start(bf16[336,512]{1,0:T(8,128)(2,1)S(1)} %collective-permute-done.7), channel_id=1, source_target_pairs={{0,120},{8,0},{16,8},{24,16},{32,24},{40,32},{48,40},{56,48},{64,5... | collective-permute-start | bytes 1032200 | tf_op jit(solution)/shard_map/ppermute | solution.py:83
  67.4 1.9 collective-permute-done.9
  69.3 5.2 %collective-permute-start.11 = (bf16[336,512]{1,0:T(8,128)(2,1)S(1)}, bf16[336,512]{1,0:T(8,128)(2,1)S(1)}, u32[]{:S(2)}, u32[]{:S(2)}) collective-permute-start(bf16[336,512]{1,0:T(8,128)(2,1)S(1)} %collective-permute-done.9), channel_id=1, source_target_pairs={{0,120},{8,0},{16,8},{24,16},{32,24},{40,32},{48,40},{56,48},{64,5... | collective-permute-start | bytes 1032200 | tf_op jit(solution)/shard_map/ppermute | solution.py:83
  76.9 1.9 collective-permute-done.11
  78.8 5.2 %collective-permute-start.13 = (bf16[336,512]{1,0:T(8,128)(2,1)S(1)}, bf16[336,512]{1,0:T(8,128)(2,1)S(1)}, u32[]{:S(2)}, u32[]{:S(2)}) collective-permute-start(bf16[336,512]{1,0:T(8,128)(2,1)S(1)} %collective-permute-done.11), channel_id=1, source_target_pairs={{0,120},{8,0},{16,8},{24,16},{32,24},{40,32},{48,40},{56,48},{64,5... | collective-permute-start | bytes 1032200 | tf_op jit(solution)/shard_map/ppermute | solution.py:83
  86.3 4.4 %collective-permute-done.13 = bf16[336,512]{1,0:T(8,128)(2,1)S(1)} collective-permute-done((bf16[336,512]{1,0:T(8,128)(2,1)S(1)}, bf16[336,512]{1,0:T(8,128)(2,1)S(1)}, u32[]{:S(2)}, u32[]{:S(2)}) %collective-permute-start.13) | collective-permute-done | bytes 344096 | tf_op jit(solution)/shard_map/ppermute | solution.py:83
  91.4 9.0 %collective-permute-done.14 = bf16[336,512]{1,0:T(8,128)(2,1)S(1)} collective-permute-done((bf16[336,512]{1,0:T(8,128)(2,1)S(1)}, bf16[336,512]{1,0:T(8,128)(2,1)S(1)}, u32[]{:S(2)}, u32[]{:S(2)}) %collective-permute-start.14) | collective-permute-done | bytes 344096 | tf_op jit(solution)/shard_map/ppermute | solution.py:74
  101.2 3.9 fusion.41
  105.3 6.8 %convolution_convert_fusion.1 = bf16[512,512]{0,1:T(8,128)(2,1)} fusion(bf16[5376,512]{1,0:T(8,128)(2,1)} %constant_dynamic-update-slice_fusion, bf16[512,5376]{0,1:T(8,128)(2,1)S(1)} %copy-done, f32[5376]{0:T(1024)S(1)} %copy-done.4, f32[512]{0:T(512)S(1)} %add_rsqrt_fusion.2), kind=kOutput, calls=%fused_computation.47 | convolution fusion | flops 2829844480 | bytes 11557888 | tf_op jit(solution)/shard_map/dot_general | solution.py:36
  112.2 2.2 collective-permute-start.15
  114.4 2.1 collective-permute-start.16
  116.5 33.9 %all-gather.7.cloned.1.call-done = bf16[5376,512]{1,0:T(8,128)(2,1)} async-done(((bf16[336,512]{1,0:T(8,128)(2,1)}), bf16[5376,512]{1,0:T(8,128)(2,1)}) %all-gather.7.cloned.1.call-update) | async-done | bytes 5505040 | tf_op jit(solution)/shard_map/all_gather | solution.py:51
  150.4 7.6 %multiply_reduce_fusion.1 = (f32[512,4]{0,1:T(4,128)S(1)}, f32[512,512]{0,1:T(8,128)S(1)}) fusion(bf16[5376,512]{1,0:T(8,128)(2,1)} %all-gather.7.cloned.1.call-done, bf16[512,5376]{0,1:T(8,128)(2,1)} %all-gather.5.cloned.1.call-done, f32[5376]{0:T(1024)S(1)} %copy-done.4, f32[512]{0:T(512)S(1)} %add_rsqrt_fusion.2), kind=kOutput, calls=%fused_computation.52 | convolution fusion | flops 2830104576 | bytes 12090368 | tf_op jit(solution)/shard_map/dot_general | solution.py:36
  159.4 8.6 %collective-permute-start.17 = (bf16[512,4,128]{2,0,1:T(8,128)(2,1)S(1)}, bf16[512,4,128]{2,0,1:T(8,128)(2,1)S(1)}, u32[]{:S(2)}, u32[]{:S(2)}) collective-permute-start(bf16[512,4,128]{2,0,1:T(8,128)(2,1)S(1)} %pad_maximum_fusion), channel_id=1, source_target_pairs={{0,16},{8,24},{16,32},{24,40},{32,48},{40,56},{48,64},{56,72},{64,... | collective-permute-start | bytes 1572872 | tf_op jit(solution)/shard_map/ppermute | solution.py:15
  168.0 1.5 collective-permute-start.18
  169.6 2.6 maximum_bitcast_fusion
  172.2 10.9 %collective-permute-done.17 = bf16[512,4,128]{2,0,1:T(8,128)(2,1)S(1)} collective-permute-done((bf16[512,4,128]{2,0,1:T(8,128)(2,1)S(1)}, bf16[512,4,128]{2,0,1:T(8,128)(2,1)S(1)}, u32[]{:S(2)}, u32[]{:S(2)}) %collective-permute-start.17) | collective-permute-done | bytes 524320 | tf_op jit(solution)/shard_map/ppermute | solution.py:15
  183.1 16.1 %collective-permute-done.18 = bf16[512,4,128]{2,0,1:T(8,128)(2,1)S(1)} collective-permute-done((bf16[512,4,128]{2,0,1:T(8,128)(2,1)S(1)}, bf16[512,4,128]{2,0,1:T(8,128)(2,1)S(1)}, u32[]{:S(2)}, u32[]{:S(2)}) %collective-permute-start.18) | collective-permute-done | bytes 524320 | tf_op jit(solution)/shard_map/ppermute | solution.py:15
  199.3 1.5 maximum_bitcast_fusion.1
  200.8 54.9 %all-gather.9.cloned.1.call-done = bf16[5376,1024]{1,0:T(8,128)(2,1)} async-done(((bf16[336,1024]{1,0:T(8,128)(2,1)}), bf16[5376,1024]{1,0:T(8,128)(2,1)}) %all-gather.9.cloned.1.call-update) | async-done | bytes 11010064 | tf_op jit(solution)/shard_map/all_gather | solution.py:50
  255.7 11.7 %convolution_bitcast_fusion = f32[64,8,8,128]{3,1,2,0:T(8,128)S(1)} fusion(bf16[5376,1024]{1,0:T(8,128)(2,1)} %all-gather.9.cloned.1.call-done, bf16[512,5376]{0,1:T(8,128)(2,1)} %all-gather.5.cloned.1.call-done, f32[5376]{0:T(1024)S(1)} %copy-done.4, f32[512]{0:T(512)S(1)} %add_rsqrt_fusion.2), kind=kOutput, calls=%fused_computation.44 | convolution fusion | flops 5648154624 | bytes 18635776 | tf_op jit(solution)/shard_map/dot_general | solution.py:36
  268.8 1.1 multiply_multiply_fusion
  272.5 46.5 %while.11 = (s32[]{:T(128)}, bf16[4,512,2,128]{1,3,2,0:T(8,128)(2,1)}, bf16[4,1536,128]{1,2,0:T(8,128)(2,1)}, bf16[4,1536,128]{2,1,0:T(8,128)(2,1)}, bf16[4,512,...) while((s32[]{:T(128)}, ...), condition=%wide.region_6.7_spmd.clone, body=%wide.region_3.6_spmd.clone.sunk | while | flops 817235456 | bytes 15486557 | solution.py:130
  272.5 1.2 fusion.74
  273.7 5.8 %fusion.75 = (f32[2,512]{1,0:T(2,128)S(1)}, f32[2,512,1536]{1,2,0:T(8,128)}) fusion(pred[512,1536]{0,1:T(8,128)(4,1)S(1)} %fusion.74, bf16[4,1536,128]{2,1,0:T(8,128)(2,1)} %get-tuple-element.159, s32[]{:T(128)} %get-tuple-element.147, bf16[4,512,2,128]{3,1,2,0:T(8,128)(2,1)S(1)} %get-tuple-element.160), kind=kOutput, calls=%fused_computation.81.clone.1 | convolution fusion | flops 407373312 | bytes 7738368 | tf_op jit(solution)/shard_map/while/body/eval_jaxpr/sub | solution.py:126
  279.6 4.3 %fusion.76 = bf16[4,512,2,128]{1,3,2,0:T(8,128)(2,1)} fusion(bf16[4,512,2,128]{1,3,2,0:T(8,128)(2,1)} %get-tuple-element.148, s32[]{:T(128)} %get-tuple-element.147, f32[2,512,1536]{1,2,0:T(8,128)} %get-tuple-element.136, f32[2,512]{1,0:T(2,128)S(1)} %get-tuple-element.137, bf16[4,1536,128]{1,2,0:T(8,128)(2,1)} %get-tuple-element.158), kind=kOutput, calls=%fused_computation.15.clone.1 | convolution fusion | flops 405929984 | bytes 6951936 | tf_op jit(solution)/shard_map/while/body/eval_jaxpr/grl,ld->rgd/dot_general | solution.py:127
  283.9 1.2 fusion.74
  285.1 5.8 %fusion.75 = (f32[2,512]{1,0:T(2,128)S(1)}, f32[2,512,1536]{1,2,0:T(8,128)}) fusion(pred[512,1536]{0,1:T(8,128)(4,1)S(1)} %fusion.74, bf16[4,1536,128]{2,1,0:T(8,128)(2,1)} %get-tuple-element.159, s32[]{:T(128)} %get-tuple-element.147, bf16[4,512,2,128]{3,1,2,0:T(8,128)(2,1)S(1)} %get-tuple-element.160), kind=kOutput, calls=%fused_computation.81.clone.1 | convolution fusion | flops 407373312 | bytes 7738368 | tf_op jit(solution)/shard_map/while/body/eval_jaxpr/sub | solution.py:126
  290.9 5.1 %fusion.76 = bf16[4,512,2,128]{1,3,2,0:T(8,128)(2,1)} fusion(bf16[4,512,2,128]{1,3,2,0:T(8,128)(2,1)} %get-tuple-element.148, s32[]{:T(128)} %get-tuple-element.147, f32[2,512,1536]{1,2,0:T(8,128)} %get-tuple-element.136, f32[2,512]{1,0:T(2,128)S(1)} %get-tuple-element.137, bf16[4,1536,128]{1,2,0:T(8,128)(2,1)} %get-tuple-element.158), kind=kOutput, calls=%fused_computation.15.clone.1 | convolution fusion | flops 405929984 | bytes 6951936 | tf_op jit(solution)/shard_map/while/body/eval_jaxpr/grl,ld->rgd/dot_general | solution.py:127
  296.0 1.2 fusion.74
  297.2 5.8 %fusion.75 = (f32[2,512]{1,0:T(2,128)S(1)}, f32[2,512,1536]{1,2,0:T(8,128)}) fusion(pred[512,1536]{0,1:T(8,128)(4,1)S(1)} %fusion.74, bf16[4,1536,128]{2,1,0:T(8,128)(2,1)} %get-tuple-element.159, s32[]{:T(128)} %get-tuple-element.147, bf16[4,512,2,128]{3,1,2,0:T(8,128)(2,1)S(1)} %get-tuple-element.160), kind=kOutput, calls=%fused_computation.81.clone.1 | convolution fusion | flops 407373312 | bytes 7738368 | tf_op jit(solution)/shard_map/while/body/eval_jaxpr/sub | solution.py:126
  303.1 4.5 %fusion.76 = bf16[4,512,2,128]{1,3,2,0:T(8,128)(2,1)} fusion(bf16[4,512,2,128]{1,3,2,0:T(8,128)(2,1)} %get-tuple-element.148, s32[]{:T(128)} %get-tuple-element.147, f32[2,512,1536]{1,2,0:T(8,128)} %get-tuple-element.136, f32[2,512]{1,0:T(2,128)S(1)} %get-tuple-element.137, bf16[4,1536,128]{1,2,0:T(8,128)(2,1)} %get-tuple-element.158), kind=kOutput, calls=%fused_computation.15.clone.1 | convolution fusion | flops 405929984 | bytes 6951936 | tf_op jit(solution)/shard_map/while/body/eval_jaxpr/grl,ld->rgd/dot_general | solution.py:127
  307.5 1.2 fusion.74
  308.7 5.8 %fusion.75 = (f32[2,512]{1,0:T(2,128)S(1)}, f32[2,512,1536]{1,2,0:T(8,128)}) fusion(pred[512,1536]{0,1:T(8,128)(4,1)S(1)} %fusion.74, bf16[4,1536,128]{2,1,0:T(8,128)(2,1)} %get-tuple-element.159, s32[]{:T(128)} %get-tuple-element.147, bf16[4,512,2,128]{3,1,2,0:T(8,128)(2,1)S(1)} %get-tuple-element.160), kind=kOutput, calls=%fused_computation.81.clone.1 | convolution fusion | flops 407373312 | bytes 7738368 | tf_op jit(solution)/shard_map/while/body/eval_jaxpr/sub | solution.py:126
  314.6 4.4 %fusion.76 = bf16[4,512,2,128]{1,3,2,0:T(8,128)(2,1)} fusion(bf16[4,512,2,128]{1,3,2,0:T(8,128)(2,1)} %get-tuple-element.148, s32[]{:T(128)} %get-tuple-element.147, f32[2,512,1536]{1,2,0:T(8,128)} %get-tuple-element.136, f32[2,512]{1,0:T(2,128)S(1)} %get-tuple-element.137, bf16[4,1536,128]{1,2,0:T(8,128)(2,1)} %get-tuple-element.158), kind=kOutput, calls=%fused_computation.15.clone.1 | convolution fusion | flops 405929984 | bytes 6951936 | tf_op jit(solution)/shard_map/while/body/eval_jaxpr/grl,ld->rgd/dot_general | solution.py:127
  319.0 21.2 %all-gather.11.cloned.1.call-done = bf16[1024,5376]{0,1:T(8,128)(2,1)} async-done(((bf16[1024,336]{0,1:T(8,128)(2,1)}), bf16[1024,5376]{0,1:T(8,128)(2,1)}) %all-gather.11.cloned.1.call-update) | async-done | bytes 11010064 | tf_op jit(solution)/shard_map/all_gather | solution.py:134
  340.2 10.4 %convolution_convert_fusion = bf16[512,5376]{0,1:T(8,128)(2,1)} fusion(bf16[1024,5376]{0,1:T(8,128)(2,1)} %all-gather.11.cloned.1.call-done, bf16[512,1024]{0,1:T(8,128)(2,1)} %bitcast.83), kind=kOutput, calls=%fused_computation.37 | convolution fusion | flops 5639897088 | bytes 17563648 | tf_op jit(solution)/shard_map/dot_general | solution.py:132
  350.6 57.3 %reduce-scatter.2.cloned.1.call-done = bf16[512,1344]{0,1:T(8,128)(2,1)} async-done(((bf16[512,5376]{0,1:T(8,128)(2,1)}), bf16[512,1344]{0,1:T(8,128)(2,1)}) %reduce-scatter.2.cloned.1.call-update) | async-done | bytes 1376272 | tf_op jit(solution)/shard_map/reduce_scatter | solution.py:137
  (75 shorter events, 21.5 us)
Async XLA Ops:
  6.5 42.9 %copy-start.1 = (bf16[336,512]{1,0:T(8,128)(2,1)S(1)}, bf16[336,512]{1,0:T(8,128)(2,1)}, u32[]{:S(2)}) copy-start(bf16[336,512]{1,0:T(8,128)(2,1)} %param.14) | copy-start | bytes 1032196
  6.5 94.6 %all-gather.5.cloned.1.call-start = ((), (), s32[]{:S(2)}) async-start(), calls=%async_computation.1 | async-start | bytes 6881280 | tf_op jit(solution)/shard_map/all_gather | solution.py:40
  7.3 143.1 %all-gather.7.cloned.1.call-start = ((), (), s32[]{:S(2)}) async-start(), calls=%async_computation.2 | async-start | bytes 5849088 | tf_op jit(solution)/shard_map/all_gather | solution.py:51
  8.0 247.7 %all-gather.9.cloned.1.call-start = ((), (), s32[]{:S(2)}) async-start(), calls=%async_computation.3 | async-start | bytes 11698176 | tf_op jit(solution)/shard_map/all_gather | solution.py:50
  8.7 331.5 %all-gather.11.cloned.1.call-start = ((), (), s32[]{:S(2)}) async-start(), calls=%async_computation.4 | async-start | bytes 11698176 | tf_op jit(solution)/shard_map/all_gather | solution.py:134
  9.3 398.6 %reduce-scatter.2.cloned.1.call-start = ((), (), s32[]{:S(2)}) async-start(), calls=%async_computation.5 | async-start | bytes 6881280 | tf_op jit(solution)/shard_map/reduce_scatter | solution.py:137
  9.4 14.8 %collective-permute-start = (bf16[336,512]{1,0:T(8,128)(2,1)}, bf16[336,512]{1,0:T(8,128)(2,1)S(1)}, u32[]{:S(2)}, u32[]{:S(2)}) collective-permute-start(bf16[336,512]{1,0:T(8,128)(2,1)} %param.14), channel_id=1, source_target_pairs={{0,8},{8,16},{16,24},{24,32},{32,40},{40,48},{48,56},{56,64},{64,7... | collective-permute-start | bytes 1032200 | tf_op jit(solution)/shard_map/ppermute | solution.py:74
  11.5 12.7 %collective-permute-start.1 = (bf16[336,512]{1,0:T(8,128)(2,1)}, bf16[336,512]{1,0:T(8,128)(2,1)S(1)}, u32[]{:S(2)}, u32[]{:S(2)}) collective-permute-start(bf16[336,512]{1,0:T(8,128)(2,1)} %param.14), channel_id=1, source_target_pairs={{0,120},{8,0},{16,8},{24,16},{32,24},{40,32},{48,40},{56,48},{64,5... | collective-permute-start | bytes 1032200 | tf_op jit(solution)/shard_map/ppermute | solution.py:83
  24.2 11.6 %collective-permute-start.2 = (bf16[336,512]{1,0:T(8,128)(2,1)S(1)}, bf16[336,512]{1,0:T(8,128)(2,1)S(1)}, u32[]{:S(2)}, u32[]{:S(2)}) collective-permute-start(bf16[336,512]{1,0:T(8,128)(2,1)S(1)} %collective-permute-done), channel_id=1, source_target_pairs={{0,8},{8,16},{16,24},{24,32},{32,40},{40,48},{48,56},{56,64},{64,7... | collective-permute-start | bytes 1032200 | tf_op jit(solution)/shard_map/ppermute | solution.py:74
  24.2 11.7 %collective-permute-start.3 = (bf16[336,512]{1,0:T(8,128)(2,1)S(1)}, bf16[336,512]{1,0:T(8,128)(2,1)S(1)}, u32[]{:S(2)}, u32[]{:S(2)}) collective-permute-start(bf16[336,512]{1,0:T(8,128)(2,1)S(1)} %collective-permute-done.1), channel_id=1, source_target_pairs={{0,120},{8,0},{16,8},{24,16},{32,24},{40,32},{48,40},{56,48},{64,5... | collective-permute-start | bytes 1032200 | tf_op jit(solution)/shard_map/ppermute | solution.py:83
  35.9 10.7 %collective-permute-start.4 = (bf16[336,512]{1,0:T(8,128)(2,1)S(1)}, bf16[336,512]{1,0:T(8,128)(2,1)S(1)}, u32[]{:S(2)}, u32[]{:S(2)}) collective-permute-start(bf16[336,512]{1,0:T(8,128)(2,1)S(1)} %collective-permute-done.2), channel_id=1, source_target_pairs={{0,8},{8,16},{16,24},{24,32},{32,40},{40,48},{48,56},{56,64},{64,7... | collective-permute-start | bytes 1032200 | tf_op jit(solution)/shard_map/ppermute | solution.py:74
  35.9 15.1 %collective-permute-start.5 = (bf16[336,512]{1,0:T(8,128)(2,1)S(1)}, bf16[336,512]{1,0:T(8,128)(2,1)S(1)}, u32[]{:S(2)}, u32[]{:S(2)}) collective-permute-start(bf16[336,512]{1,0:T(8,128)(2,1)S(1)} %collective-permute-done.3), channel_id=1, source_target_pairs={{0,120},{8,0},{16,8},{24,16},{32,24},{40,32},{48,40},{56,48},{64,5... | collective-permute-start | bytes 1032200 | tf_op jit(solution)/shard_map/ppermute | solution.py:83
  46.6 9.9 %collective-permute-start.6 = (bf16[336,512]{1,0:T(8,128)(2,1)S(1)}, bf16[336,512]{1,0:T(8,128)(2,1)S(1)}, u32[]{:S(2)}, u32[]{:S(2)}) collective-permute-start(bf16[336,512]{1,0:T(8,128)(2,1)S(1)} %collective-permute-done.4), channel_id=1, source_target_pairs={{0,8},{8,16},{16,24},{24,32},{32,40},{40,48},{48,56},{56,64},{64,7... | collective-permute-start | bytes 1032200 | tf_op jit(solution)/shard_map/ppermute | solution.py:74
  50.9 9.0 %collective-permute-start.7 = (bf16[336,512]{1,0:T(8,128)(2,1)S(1)}, bf16[336,512]{1,0:T(8,128)(2,1)S(1)}, u32[]{:S(2)}, u32[]{:S(2)}) collective-permute-start(bf16[336,512]{1,0:T(8,128)(2,1)S(1)} %collective-permute-done.5), channel_id=1, source_target_pairs={{0,120},{8,0},{16,8},{24,16},{32,24},{40,32},{48,40},{56,48},{64,5... | collective-permute-start | bytes 1032200 | tf_op jit(solution)/shard_map/ppermute | solution.py:83
  56.5 9.4 %collective-permute-start.8 = (bf16[336,512]{1,0:T(8,128)(2,1)S(1)}, bf16[336,512]{1,0:T(8,128)(2,1)S(1)}, u32[]{:S(2)}, u32[]{:S(2)}) collective-permute-start(bf16[336,512]{1,0:T(8,128)(2,1)S(1)} %collective-permute-done.6), channel_id=1, source_target_pairs={{0,8},{8,16},{16,24},{24,32},{32,40},{40,48},{48,56},{56,64},{64,7... | collective-permute-start | bytes 1032200 | tf_op jit(solution)/shard_map/ppermute | solution.py:74
  59.9 9.4 %collective-permute-start.9 = (bf16[336,512]{1,0:T(8,128)(2,1)S(1)}, bf16[336,512]{1,0:T(8,128)(2,1)S(1)}, u32[]{:S(2)}, u32[]{:S(2)}) collective-permute-start(bf16[336,512]{1,0:T(8,128)(2,1)S(1)} %collective-permute-done.7), channel_id=1, source_target_pairs={{0,120},{8,0},{16,8},{24,16},{32,24},{40,32},{48,40},{56,48},{64,5... | collective-permute-start | bytes 1032200 | tf_op jit(solution)/shard_map/ppermute | solution.py:83
  65.9 9.4 %collective-permute-start.10 = (bf16[336,512]{1,0:T(8,128)(2,1)S(1)}, bf16[336,512]{1,0:T(8,128)(2,1)S(1)}, u32[]{:S(2)}, u32[]{:S(2)}) collective-permute-start(bf16[336,512]{1,0:T(8,128)(2,1)S(1)} %collective-permute-done.8), channel_id=1, source_target_pairs={{0,8},{8,16},{16,24},{24,32},{32,40},{40,48},{48,56},{56,64},{64,7... | collective-permute-start | bytes 1032200 | tf_op jit(solution)/shard_map/ppermute | solution.py:74
  67.4 37.6 %copy-start.4 = (f32[5376]{0:T(1024)S(1)}, f32[5376]{0:T(1024)}, u32[]{:S(2)}) copy-start(f32[5376]{0:T(1024)} %param.11) | copy-start | bytes 64516
  69.3 9.4 %collective-permute-start.11 = (bf16[336,512]{1,0:T(8,128)(2,1)S(1)}, bf16[336,512]{1,0:T(8,128)(2,1)S(1)}, u32[]{:S(2)}, u32[]{:S(2)}) collective-permute-start(bf16[336,512]{1,0:T(8,128)(2,1)S(1)} %collective-permute-done.9), channel_id=1, source_target_pairs={{0,120},{8,0},{16,8},{24,16},{32,24},{40,32},{48,40},{56,48},{64,5... | collective-permute-start | bytes 1032200 | tf_op jit(solution)/shard_map/ppermute | solution.py:83
  75.3 9.4 %collective-permute-start.12 = (bf16[336,512]{1,0:T(8,128)(2,1)S(1)}, bf16[336,512]{1,0:T(8,128)(2,1)S(1)}, u32[]{:S(2)}, u32[]{:S(2)}) collective-permute-start(bf16[336,512]{1,0:T(8,128)(2,1)S(1)} %collective-permute-done.10), channel_id=1, source_target_pairs={{0,8},{8,16},{16,24},{24,32},{32,40},{40,48},{48,56},{56,64},{64,7... | collective-permute-start | bytes 1032200 | tf_op jit(solution)/shard_map/ppermute | solution.py:74
  78.8 11.9 %collective-permute-start.13 = (bf16[336,512]{1,0:T(8,128)(2,1)S(1)}, bf16[336,512]{1,0:T(8,128)(2,1)S(1)}, u32[]{:S(2)}, u32[]{:S(2)}) collective-permute-start(bf16[336,512]{1,0:T(8,128)(2,1)S(1)} %collective-permute-done.11), channel_id=1, source_target_pairs={{0,120},{8,0},{16,8},{24,16},{32,24},{40,32},{48,40},{56,48},{64,5... | collective-permute-start | bytes 1032200 | tf_op jit(solution)/shard_map/ppermute | solution.py:83
  84.8 15.6 %collective-permute-start.14 = (bf16[336,512]{1,0:T(8,128)(2,1)S(1)}, bf16[336,512]{1,0:T(8,128)(2,1)S(1)}, u32[]{:S(2)}, u32[]{:S(2)}) collective-permute-start(bf16[336,512]{1,0:T(8,128)(2,1)S(1)} %collective-permute-done.12), channel_id=1, source_target_pairs={{0,8},{8,16},{16,24},{24,32},{32,40},{40,48},{48,56},{56,64},{64,7... | collective-permute-start | bytes 1032200 | tf_op jit(solution)/shard_map/ppermute | solution.py:74
  101.2 4.2 %copy-start = (bf16[512,5376]{0,1:T(8,128)(2,1)S(1)}, bf16[512,5376]{0,1:T(8,128)(2,1)}, u32[]{:S(2)}) copy-start(bf16[512,5376]{0,1:T(8,128)(2,1)} %all-gather.5.cloned.1.call-done) | copy-start | bytes 16515076
  112.2 46.1 %copy-start.2 = (f32[128]{0:T(128)S(1)}, f32[128]{0:T(128)}, u32[]{:S(2)}) copy-start(f32[128]{0:T(128)} %param.16) | copy-start | bytes 1540
  112.2 57.4 %collective-permute-start.15 = (bf16[512,4,128]{0,2,1:T(8,128)(2,1)}, bf16[512,4,128]{0,2,1:T(8,128)(2,1)}, u32[]{:S(2)}, u32[]{:S(2)}) collective-permute-start(bf16[512,4,128]{0,2,1:T(8,128)(2,1)} %bitcast), channel_id=1, source_target_pairs={{0,16},{8,24},{16,32},{24,40},{32,48},{40,56},{48,64},{56,72},{64,... | collective-permute-start | bytes 1572872 | tf_op jit(solution)/shard_map/ppermute | solution.py:15
  114.4 55.2 %collective-permute-start.16 = (bf16[512,4,128]{0,2,1:T(8,128)(2,1)}, bf16[512,4,128]{0,2,1:T(8,128)(2,1)}, u32[]{:S(2)}, u32[]{:S(2)}) collective-permute-start(bf16[512,4,128]{0,2,1:T(8,128)(2,1)} %bitcast), channel_id=1, source_target_pairs={{0,8},{8,16},{16,24},{24,32},{32,40},{40,48},{48,56},{56,64},{64,7... | collective-permute-start | bytes 1572872 | tf_op jit(solution)/shard_map/ppermute | solution.py:15
  159.4 23.7 %collective-permute-start.17 = (bf16[512,4,128]{2,0,1:T(8,128)(2,1)S(1)}, bf16[512,4,128]{2,0,1:T(8,128)(2,1)S(1)}, u32[]{:S(2)}, u32[]{:S(2)}) collective-permute-start(bf16[512,4,128]{2,0,1:T(8,128)(2,1)S(1)} %pad_maximum_fusion), channel_id=1, source_target_pairs={{0,16},{8,24},{16,32},{24,40},{32,48},{40,56},{48,64},{56,72},{64,... | collective-permute-start | bytes 1572872 | tf_op jit(solution)/shard_map/ppermute | solution.py:15
  168.0 31.3 %collective-permute-start.18 = (bf16[512,4,128]{2,0,1:T(8,128)(2,1)S(1)}, bf16[512,4,128]{2,0,1:T(8,128)(2,1)S(1)}, u32[]{:S(2)}, u32[]{:S(2)}) collective-permute-start(bf16[512,4,128]{2,0,1:T(8,128)(2,1)S(1)} %pad_maximum_fusion), channel_id=1, source_target_pairs={{0,8},{8,16},{16,24},{24,32},{32,40},{40,48},{48,56},{56,64},{64,7... | collective-permute-start | bytes 1572872 | tf_op jit(solution)/shard_map/ppermute | solution.py:15
  267.4 1.4 copy-start.3
Sparse Core Ops, SparseCore 0:
  9.0 62.3 all-gather.4
  73.5 76.7 all-gather.6
  152.5 103.1 all-gather.8
  257.7 82.4 all-gather.10
  350.8 57.1 reduce-scatter.1
